TPU v7x, 128 devices: a whole 4x4x4 slice. The times are simulated.
128 devices in a mesh: section: 2 (over z_hi), seq: 8 (over x, z_lo), expert: 8 (over y, core).
Axes of the slice: x: 4, y: 4, z: 4 (z_hi: 2, z_lo: 2; z = z_hi * 2 + z_lo), core: 2. Of those that a mesh axis runs over, the one named last changes fastest.
Arguments:
- tokens: bfloat16 [2, 1024, 2048], P(None, ('seq', 'expert')), may hold values from -12 to 12
- prompt_lengths: int32 [2, 3], replicated, may hold values from 1 to 512, 1024 in all within a row
- cache_lengths: int32 [2, 3], replicated, may hold values from 1 to 1024, 2048 in all within a row
- kv_cache: bfloat16 [2, 2048, 2, 2048], P(None, 'seq', None, 'expert'), may hold values from -360 to 360
- attn_routes: int32 [2, 1024, 2], P(None, 'seq'), may hold values from 0 to 3, all different within a row
- ffn_routes: int32 [2, 1024, 2], P(None, ('seq', 'expert')), may hold values from 0 to 7, all different within a row; in each aligned block of 16 rows (0 to 15, 16 to 31, ..., all dimensions but the last counted through in order) at most 8 rows name the same one
- attn_gain: float32 [2048], replicated, may hold values from 0.1 to 1.9
- ffn_gain: float32 [2048], replicated, may hold values from 0.1 to 1.9
- attn_mix: bfloat16 [2048, 4], replicated, may hold values from -0.125 to 0.125
- query_weight: bfloat16 [2048, 4, 2048], P(None, None, 'expert'), may hold values from -0.125 to 0.125
- kv_weight: bfloat16 [2048, 2, 2048], P(None, None, 'expert'), may hold values from -0.125 to 0.125
- out_weight: bfloat16 [4, 2048, 2048], P(None, 'expert'), may hold values from -0.125 to 0.125
- ffn_mix: bfloat16 [2048, 8], replicated, may hold values from -0.125 to 0.125
- in_weight: bfloat16 [8, 2048, 2, 5632], P('expert', None, None, 'seq'), may hold values from -0.125 to 0.125
- down_weight: bfloat16 [8, 5632, 2048], P('expert', 'seq'), may hold values from -0.078125 to 0.078125
Outputs:
- layer_out: bfloat16 [2, 1024, 2048], P('section', ('seq', 'expert'))
Inputs may be any that keep to these rules, and one draw needn't show every extreme that they name: `prompt_lengths`: each row sums to 1024; its largest entry is 512. `cache_lengths`: each row sums to 2048; its largest entry is 1024. `attn_routes`: the two experts of a position differ; every expert is named somewhere. `ffn_routes`: the two experts of a position differ. Taking all micro-batches and positions in order, in each aligned block of 16 positions (the rows of one device) no expert is named more than 8 times, and some block names one exactly 8 times.
All inputs are finite; a program needn't handle non-finite values.
Results may differ from a plain program's by a relative error of at most 0.029.
Values may be sent and summed in bfloat16 or wider, within the bound.
A program may use at most 128 MiB of HBM per device.

v0:
```python
import jax
import jax.numpy as jnp
from jax import lax
from jax.sharding import PartitionSpec as P

HEAD_DIM = 128


EPS = 1e-06
THETA = 10000.0
NEGATIVE = -1e30


def passed_along(value, axis, steps):
    count = lax.axis_size(axis)
    initial, last = (max(0, -steps), min(count, count - steps))
    return lax.ppermute(value, axis, [(source, source + steps) for source in range(initial, last)])


def rms_scale(values, gain):
    widened = values.astype(jnp.float32)
    inverse = lax.rsqrt(jnp.mean(widened * widened, axis=-1, keepdims=True) + EPS)
    return (widened * inverse * gain).astype(jnp.bfloat16)


def segment_of(row_index, lengths):
    ends = jnp.cumsum(lengths)
    return jnp.sum((row_index[:, None] >= ends[None, :]).astype(jnp.int32), axis=1)


def positions(row_index, lengths, cached):
    ends = jnp.cumsum(lengths)
    segment = jnp.sum((row_index[:, None] >= ends[None, :]).astype(jnp.int32), axis=1)
    matched = segment[:, None] == jnp.arange(lengths.shape[0], dtype=jnp.int32)[None, :]
    begins = jnp.sum(jnp.where(matched, (ends - lengths)[None, :], 0), axis=1)
    offsets = jnp.sum(jnp.where(matched, cached[None, :], 0), axis=1)
    return (segment, offsets + row_index - begins)


def rotate(values, place):
    half_dim = values.shape[-1] // 2
    freq = THETA ** (-jnp.arange(half_dim, dtype=jnp.float32) / half_dim)
    angle = place.astype(jnp.float32)[:, None] * freq[None, :]
    shape = (values.shape[0],) + (1,) * (values.ndim - 2) + (half_dim,)
    cosine = jnp.cos(angle).reshape(shape)
    sine = jnp.sin(angle).reshape(shape)
    former = values[..., :half_dim]
    latter = values[..., half_dim:]
    return jnp.concatenate(
        [former * cosine - latter * sine, latter * cosine + former * sine], axis=-1
    )


def route_gates(normed, mixing, routes):
    logits = jnp.dot(normed, mixing, preferred_element_type=jnp.float32)
    chosen = jnp.take_along_axis(logits, routes, axis=1)
    leading = jax.nn.sigmoid(chosen[:, 0] - chosen[:, 1])
    return jnp.stack([leading, 1.0 - leading], axis=1)


def select_batch(values, batch):
    return lax.dynamic_index_in_dim(values, batch, 0, keepdims=False)


def attention_block(
    own_rows, lengths, cached, cache_rows, routes, gain, mixing, query_weight, kv_weight, out_weight
):
    gathered = lax.all_gather(own_rows, "expert", axis=0, tiled=True)
    count = gathered.shape[0]
    normed = rms_scale(gathered, gain)
    row_index = lax.axis_index("seq") * count + jnp.arange(count, dtype=jnp.int32)
    segment, place = positions(row_index, lengths, cached)
    gates = route_gates(normed, mixing, routes)
    experts = query_weight.shape[1]
    width = query_weight.shape[2]
    local_heads = width // HEAD_DIM
    query_all = jnp.dot(
        normed, query_weight.reshape(query_weight.shape[0], -1), preferred_element_type=jnp.float32
    )
    query_all = query_all.reshape(count, experts, local_heads, HEAD_DIM)
    query = jnp.take_along_axis(query_all, routes[:, :, None, None], axis=1)
    query = rotate(query, place).astype(jnp.bfloat16)
    queries = query.reshape(count * 2, local_heads, HEAD_DIM)
    projected = jnp.dot(
        normed, kv_weight.reshape(kv_weight.shape[0], -1), preferred_element_type=jnp.float32
    )
    projected = projected.reshape(count, 2, local_heads, HEAD_DIM)
    fresh_keys = rotate(projected[:, 0], place).astype(jnp.bfloat16).reshape(count, width)
    fresh_values = projected[:, 1].astype(jnp.bfloat16).reshape(count, width)
    fresh = jnp.stack([fresh_keys, fresh_values], axis=1)
    query_segment = jnp.repeat(segment, 2)
    query_index = jnp.repeat(row_index, 2)
    scale = HEAD_DIM ** (-0.5)
    slots = count * 2

    def absorb(carried, piece, allowed):
        row_top, row_total, row_sum = carried
        keys = piece[:, 0].reshape(-1, local_heads, HEAD_DIM)
        values = piece[:, 1].reshape(-1, local_heads, HEAD_DIM)
        scores = (
            jnp.einsum("qhd,khd->hqk", queries, keys, preferred_element_type=jnp.float32) * scale
        )
        scores = jnp.where(allowed[None], scores, NEGATIVE)
        new_top = jnp.maximum(row_top, jnp.max(scores, axis=2))
        weights = jnp.where(allowed[None], jnp.exp(scores - new_top[:, :, None]), 0.0)
        shrink = jnp.exp(row_top - new_top)
        row_total = row_total * shrink + jnp.sum(weights, axis=2)
        row_sum = row_sum * shrink[:, :, None] + jnp.einsum(
            "hqk,khd->hqd", weights.astype(jnp.bfloat16), values, preferred_element_type=jnp.float32
        )
        return (new_top, row_total, row_sum)

    initial = (
        jnp.full((local_heads, slots), NEGATIVE, jnp.float32),
        jnp.zeros((local_heads, slots), jnp.float32),
        jnp.zeros((local_heads, slots, HEAD_DIM), jnp.float32),
    )
    piece = lax.all_gather(cache_rows, "seq", axis=0, tiled=True)
    key_segment = segment_of(jnp.arange(piece.shape[0], dtype=jnp.int32), cached)
    allowed = query_segment[:, None] == key_segment[None, :]
    carried = absorb(initial, piece, allowed)
    piece = lax.all_gather(fresh, "seq", axis=0, tiled=True)
    key_index = jnp.arange(piece.shape[0], dtype=jnp.int32)
    key_segment = segment_of(key_index, lengths)
    allowed = (query_segment[:, None] == key_segment[None, :]) & (
        key_index[None, :] <= query_index[:, None]
    )
    row_top, row_total, row_sum = absorb(carried, piece, allowed)
    attended = (row_sum / row_total[:, :, None]).astype(jnp.bfloat16)
    attended = attended.transpose(1, 0, 2).reshape(count, 2, width)
    select = (routes[:, :, None] == jnp.arange(experts, dtype=jnp.int32)[None, None, :]).astype(
        jnp.float32
    )
    select = select * gates[:, :, None]
    spread = jnp.einsum("tka,tkd->tad", select, attended.astype(jnp.float32)).astype(jnp.bfloat16)
    spread = spread.reshape(count, experts * width)
    out_flat = out_weight.reshape(experts * width, -1)
    term = lax.psum_scatter(
        jnp.dot(spread, out_flat, preferred_element_type=jnp.float32).astype(jnp.bfloat16),
        "expert",
        scatter_dimension=0,
        tiled=True,
    ).astype(jnp.float32)
    return (own_rows.astype(jnp.float32) + term).astype(jnp.bfloat16)


def expert_hidden(rows, in_weight):
    single = in_weight[0]
    both = jnp.dot(rows, single.reshape(single.shape[0], -1), preferred_element_type=jnp.float32)
    both = both.reshape(rows.shape[0], 2, -1)
    return (jax.nn.silu(both[:, 0]) * both[:, 1]).astype(jnp.bfloat16)


def expert_block(middle, routes, gain, mixing, in_weight, down_weight):
    rows = middle.shape[0]
    features = middle.shape[1]
    normed = rms_scale(middle, gain)
    gates = route_gates(normed, mixing, routes)
    experts = mixing.shape[1]
    capacity = max(2, 4 * rows // experts)
    flat = routes.reshape(-1)
    member = (flat[:, None] == jnp.arange(experts, dtype=jnp.int32)[None, :]).astype(jnp.int32)
    earlier = jnp.cumsum(member, axis=0) - member
    slot = jnp.sum(earlier * member, axis=1)
    target = flat * capacity + slot
    table = (jnp.arange(experts * capacity, dtype=jnp.int32)[:, None] == target[None, :]).astype(
        jnp.bfloat16
    )
    table = jnp.sum(table.reshape(experts * capacity, rows, 2), axis=2)
    buffer = jnp.dot(table, normed, preferred_element_type=jnp.float32).astype(jnp.bfloat16)
    buffer = buffer.reshape(experts, capacity, features)
    seq_count = lax.axis_size("seq")
    copies = jnp.broadcast_to(buffer[None], (seq_count,) + buffer.shape)
    copies = copies.reshape(seq_count * experts, capacity, features)
    arrived = lax.all_to_all(copies, ("seq", "expert"), split_axis=0, concat_axis=0, tiled=True)
    flat_rows = arrived.reshape(-1, features)
    hidden = expert_hidden(flat_rows, in_weight)
    partial_value = jnp.dot(hidden, down_weight[0], preferred_element_type=jnp.float32)
    partial_value = partial_value.astype(jnp.bfloat16).reshape(arrived.shape)
    returned = lax.all_to_all(
        partial_value, ("seq", "expert"), split_axis=0, concat_axis=0, tiled=True
    )
    results = jnp.sum(
        returned.reshape(seq_count, experts, capacity, features).astype(jnp.float32), axis=0
    )
    picked = jnp.take(results.reshape(experts * capacity, features), target, axis=0).reshape(
        rows, 2, features
    )
    mixture = gates[:, 0:1] * picked[:, 0] + gates[:, 1:2] * picked[:, 1]
    return (middle.astype(jnp.float32) + mixture).astype(jnp.bfloat16)


def on_device(
    tokens,
    prompt_lengths,
    cache_lengths,
    kv_cache,
    attn_routes,
    ffn_routes,
    attn_gain,
    ffn_gain,
    attn_mix,
    query_weight,
    kv_weight,
    out_weight,
    ffn_mix,
    in_weight,
    down_weight,
):
    batches = tokens.shape[0]
    half_count = batches // 2
    section = lax.axis_index("section")

    def attend(batch):
        return attention_block(
            select_batch(tokens, batch),
            select_batch(prompt_lengths, batch),
            select_batch(cache_lengths, batch),
            select_batch(kv_cache, batch),
            select_batch(attn_routes, batch),
            attn_gain,
            attn_mix,
            query_weight,
            kv_weight,
            out_weight,
        )

    def finish(middle, batch):
        return expert_block(
            middle, select_batch(ffn_routes, batch), ffn_gain, ffn_mix, in_weight, down_weight
        )

    blank = jnp.zeros(tokens.shape[1:], jnp.bfloat16)
    first_section = section == 0

    def one_tick(incoming, tick):
        ahead = jnp.minimum(tick, batches - 1)
        behind = jnp.maximum(tick - 1, 0)
        attended_rows = attend(ahead)
        finished_rows = finish(incoming, behind)
        produced = jnp.where(first_section, attended_rows, finished_rows)
        passed = passed_along(produced, "section", 1)
        return (passed, produced)

    ticks = jnp.arange(batches + 1, dtype=jnp.int32)
    _, produced_all = lax.scan(one_tick, blank, ticks)
    finished = produced_all[1:]
    former_half = finished[:half_count]
    latter_half = finished[half_count:]
    returned = passed_along(former_half, "section", -1)
    return jnp.where(first_section, returned, latter_half)


def solution(mesh):
    return jax.shard_map(
        on_device,
        mesh=mesh,
        in_specs=(
            P(None, ("seq", "expert"), None),
            P(),
            P(),
            P(None, "seq", None, "expert"),
            P(None, "seq", None),
            P(None, ("seq", "expert"), None),
            P(),
            P(),
            P(),
            P(None, None, "expert"),
            P(None, None, "expert"),
            P(None, "expert", None),
            P(),
            P("expert", None, None, "seq"),
            P("expert", "seq", None),
        ),
        out_specs=P("section", ("seq", "expert"), None),
        check_vma=False,
    )
```

profile of v0, /device:TPU:1, one launch (start us, length us, event | category | flops | bytes accessed | tf_op | source)
XLA Modules:
  0.0 692.4 jit_solution(16072841294543308900)
XLA Ops:
  6.5 7.7 %copy.140 = bf16[2048,4,256]{0,2,1:T(8,128)(2,1)} copy(bf16[2048,4,256]{2,1,0:T(4,128)(2,1)} %param.26) | data formatting | bytes 8388608 | tf_op jit(solution)/shard_map/while | solution.py:246
  14.3 4.8 copy.142
  19.2 657.8 %while.14 = (s32[]{:T(128)}, bf16[16,2048]{1,0:T(8,128)(2,1)S(1)}, bf16[3,16,2048]{2,1,0:T(8,128)(2,1)}, pred[]{:T(512)}, s32[3]{0:T(128)S(1)}, /*index=5*/bf16[...) while((s32[]{:T(128)}, bf16[16,2048]{1,0:T(8,128)(2,1)S(1)}, ...), condition=%wide.region_19.20_spmd, body=%wide.region_0.19_spmd.sunk | while | flops 6617626624 | bytes 126714792 | solution.py:246
  20.5 15.0 %all-gather.5 = bf16[1,128,2048]{2,1,0:T(8,128)(2,1)S(1)} all-gather(bf16[1,16,2048]{2,1,0:T(8,128)(2,1)S(1)} %constant_dynamic-slice_fusion.10), channel_id=2, replica_groups=mesh['section'=2,'seq'=8,'expert'=8] {'expert'}, dimensions={1}, use_global_device_ids=true | all-gather | bytes 589824 | tf_op jit(solution)/shard_map/while/body/eval_jaxpr/all_gather | solution.py:68
  42.9 8.5 %all-to-all-start = ((bf16[64,8,2048]{2,1,0:T(8,128)(2,1)}), bf16[64,8,2048]{2,1,0:T(8,128)(2,1)}, u32[]{:S(2)}, u32[]{:S(2)}) async-start(bf16[64,8,2048]{2,1,0:T(8,128)(2,1)} %bitcast.287), calls=%async_computation | async-start | bytes 4194304 | tf_op jit(solution)/shard_map/while/body/eval_jaxpr/all_to_all | solution.py:175
  55.4 3.8 fusion.202
  66.4 33.4 %all-gather.11.cloned.1.call-done = bf16[1024,2,256]{0,2,1:T(8,128)(2,1)} async-done(((bf16[128,2,256]{0,2,1:T(8,128)(2,1)}), bf16[1024,2,256]{0,2,1:T(8,128)(2,1)}) %all-gather.11.cloned.1.call-update) | async-done | bytes 1048592 | tf_op jit(solution)/shard_map/while/body/eval_jaxpr/all_gather | solution.py:122
  103.8 6.0 fusion.195
  113.3 13.6 %all-to-all-start.1 = ((bf16[64,8,2048]{2,1,0:T(8,128)(2,1)}), bf16[64,8,2048]{2,1,0:T(8,128)(2,1)S(1)}, u32[]{:S(2)}, u32[]{:S(2)}) async-start(bf16[64,8,2048]{2,1,0:T(8,128)(2,1)} %fusion.196), calls=%async_computation.1 | async-start | bytes 4194304 | tf_op jit(solution)/shard_map/while/body/eval_jaxpr/all_to_all | solution.py:180
  127.0 57.7 %all-gather.9.cloned.1.call-done = bf16[1,2048,2,256]{1,3,2,0:T(8,128)(2,1)} async-done(((bf16[1,256,2,256]{1,3,2,0:T(8,128)(2,1)}), bf16[1,2048,2,256]{1,3,2,0:T(8,128)(2,1)}) %all-gather.9.cloned.1.call-update) | async-done | bytes 2097168 | tf_op jit(solution)/shard_map/while/body/eval_jaxpr/all_gather | solution.py:118
  193.4 3.7 fusion.216
  198.5 32.1 %reduce-scatter.2.cloned.1.call-done = bf16[16,2048]{1,0:T(8,128)(2,1)} async-done(((bf16[128,2048]{1,0:T(8,128)(2,1)}), bf16[16,2048]{1,0:T(8,128)(2,1)}) %reduce-scatter.2.cloned.1.call-update) | async-done | bytes 65552 | tf_op jit(solution)/shard_map/while/body/eval_jaxpr/reduce_scatter | solution.py:138
  232.2 4.9 collective-permute-start
  239.6 17.1 %all-gather.5 = bf16[1,128,2048]{2,1,0:T(8,128)(2,1)S(1)} all-gather(bf16[1,16,2048]{2,1,0:T(8,128)(2,1)S(1)} %constant_dynamic-slice_fusion.10), channel_id=2, replica_groups=mesh['section'=2,'seq'=8,'expert'=8] {'expert'}, dimensions={1}, use_global_device_ids=true | all-gather | bytes 589824 | tf_op jit(solution)/shard_map/while/body/eval_jaxpr/all_gather | solution.py:68
  264.1 6.1 all-to-all-start
  274.2 3.7 fusion.202
  285.2 35.7 %all-gather.11.cloned.1.call-done = bf16[1024,2,256]{0,2,1:T(8,128)(2,1)} async-done(((bf16[128,2,256]{0,2,1:T(8,128)(2,1)}), bf16[1024,2,256]{0,2,1:T(8,128)(2,1)}) %all-gather.11.cloned.1.call-update) | async-done | bytes 1048592 | tf_op jit(solution)/shard_map/while/body/eval_jaxpr/all_gather | solution.py:122
  325.0 6.0 fusion.195
  334.4 13.3 %all-to-all-start.1 = ((bf16[64,8,2048]{2,1,0:T(8,128)(2,1)}), bf16[64,8,2048]{2,1,0:T(8,128)(2,1)S(1)}, u32[]{:S(2)}, u32[]{:S(2)}) async-start(bf16[64,8,2048]{2,1,0:T(8,128)(2,1)} %fusion.196), calls=%async_computation.1 | async-start | bytes 4194304 | tf_op jit(solution)/shard_map/while/body/eval_jaxpr/all_to_all | solution.py:180
  347.7 62.6 %all-gather.9.cloned.1.call-done = bf16[1,2048,2,256]{1,3,2,0:T(8,128)(2,1)} async-done(((bf16[1,256,2,256]{1,3,2,0:T(8,128)(2,1)}), bf16[1,2048,2,256]{1,3,2,0:T(8,128)(2,1)}) %all-gather.9.cloned.1.call-update) | async-done | bytes 2097168 | tf_op jit(solution)/shard_map/while/body/eval_jaxpr/all_gather | solution.py:118
  424.2 24.7 %reduce-scatter.2.cloned.1.call-done = bf16[16,2048]{1,0:T(8,128)(2,1)} async-done(((bf16[128,2048]{1,0:T(8,128)(2,1)}), bf16[16,2048]{1,0:T(8,128)(2,1)}) %reduce-scatter.2.cloned.1.call-update) | async-done | bytes 65552 | tf_op jit(solution)/shard_map/while/body/eval_jaxpr/reduce_scatter | solution.py:138
  450.5 4.8 collective-permute-start
  457.9 17.1 %all-gather.5 = bf16[1,128,2048]{2,1,0:T(8,128)(2,1)S(1)} all-gather(bf16[1,16,2048]{2,1,0:T(8,128)(2,1)S(1)} %constant_dynamic-slice_fusion.10), channel_id=2, replica_groups=mesh['section'=2,'seq'=8,'expert'=8] {'expert'}, dimensions={1}, use_global_device_ids=true | all-gather | bytes 589824 | tf_op jit(solution)/shard_map/while/body/eval_jaxpr/all_gather | solution.py:68
  482.3 6.2 all-to-all-start
  503.5 35.7 %all-gather.11.cloned.1.call-done = bf16[1024,2,256]{0,2,1:T(8,128)(2,1)} async-done(((bf16[128,2,256]{0,2,1:T(8,128)(2,1)}), bf16[1024,2,256]{0,2,1:T(8,128)(2,1)}) %all-gather.11.cloned.1.call-update) | async-done | bytes 1048592 | tf_op jit(solution)/shard_map/while/body/eval_jaxpr/all_gather | solution.py:122
  543.4 6.0 fusion.195
  552.8 13.3 %all-to-all-start.1 = ((bf16[64,8,2048]{2,1,0:T(8,128)(2,1)}), bf16[64,8,2048]{2,1,0:T(8,128)(2,1)S(1)}, u32[]{:S(2)}, u32[]{:S(2)}) async-start(bf16[64,8,2048]{2,1,0:T(8,128)(2,1)} %fusion.196), calls=%async_computation.1 | async-start | bytes 4194304 | tf_op jit(solution)/shard_map/while/body/eval_jaxpr/all_to_all | solution.py:180
  566.1 58.4 %all-gather.9.cloned.1.call-done = bf16[1,2048,2,256]{1,3,2,0:T(8,128)(2,1)} async-done(((bf16[1,256,2,256]{1,3,2,0:T(8,128)(2,1)}), bf16[1,2048,2,256]{1,3,2,0:T(8,128)(2,1)}) %all-gather.9.cloned.1.call-update) | async-done | bytes 2097168 | tf_op jit(solution)/shard_map/while/body/eval_jaxpr/all_gather | solution.py:118
  633.3 3.7 fusion.216
  638.4 30.9 %reduce-scatter.2.cloned.1.call-done = bf16[16,2048]{1,0:T(8,128)(2,1)} async-done(((bf16[128,2048]{1,0:T(8,128)(2,1)}), bf16[16,2048]{1,0:T(8,128)(2,1)}) %reduce-scatter.2.cloned.1.call-update) | async-done | bytes 65552 | tf_op jit(solution)/shard_map/while/body/eval_jaxpr/reduce_scatter | solution.py:138
  670.9 4.8 collective-permute-start
  679.2 5.2 collective-permute-done.1
  (355 shorter events, 127.3 us)
Async XLA Ops:
  6.5 7.7 %copy-start.3 = (bf16[2048,2,256]{2,1,0:T(2,128)(2,1)S(1)}, bf16[2048,2,256]{2,1,0:T(2,128)(2,1)}, u32[]{:S(2)}) copy-start(bf16[2048,2,256]{2,1,0:T(2,128)(2,1)} %param.27) | copy-start | bytes 6291460
  14.2 4.9 copy-start.2
  14.2 4.9 copy-start.4
  14.2 4.9 copy-start.5
  14.3 4.9 copy-start.6
  14.3 4.9 copy-start.7
  14.3 4.9 copy-start.8
  14.3 4.9 copy-start.9
  14.3 4.9 copy-start.11
  14.3 4.9 copy-start.12
  19.2 80.5 %all-gather.11.cloned.1.call-start = ((), (), s32[]{:S(2)}) async-start(), calls=%async_computation.4 | async-start | bytes 1179648 | tf_op jit(solution)/shard_map/while/body/eval_jaxpr/all_gather | solution.py:122
  42.9 61.0 %all-to-all-start = ((bf16[64,8,2048]{2,1,0:T(8,128)(2,1)}), bf16[64,8,2048]{2,1,0:T(8,128)(2,1)}, u32[]{:S(2)}, u32[]{:S(2)}) async-start(bf16[64,8,2048]{2,1,0:T(8,128)(2,1)} %bitcast.287), calls=%async_computation | async-start | bytes 4194304 | tf_op jit(solution)/shard_map/while/body/eval_jaxpr/all_to_all | solution.py:175
  51.4 133.3 %all-gather.9.cloned.1.call-start = ((), (), s32[]{:S(2)}) async-start(), calls=%async_computation.3 | async-start | bytes 2359296 | tf_op jit(solution)/shard_map/while/body/eval_jaxpr/all_gather | solution.py:118
  103.8 6.1 copy-start.10
  113.3 83.9 %all-to-all-start.1 = ((bf16[64,8,2048]{2,1,0:T(8,128)(2,1)}), bf16[64,8,2048]{2,1,0:T(8,128)(2,1)S(1)}, u32[]{:S(2)}, u32[]{:S(2)}) async-start(bf16[64,8,2048]{2,1,0:T(8,128)(2,1)} %fusion.196), calls=%async_computation.1 | async-start | bytes 4194304 | tf_op jit(solution)/shard_map/while/body/eval_jaxpr/all_to_all | solution.py:180
  126.9 103.7 %reduce-scatter.2.cloned.1.call-start = ((), (), s32[]{:S(2)}) async-start(), calls=%async_computation.5 | async-start | bytes 589824 | tf_op jit(solution)/shard_map/while/body/eval_jaxpr/reduce_scatter | solution.py:138
  232.2 6.2 collective-permute-start
  238.3 82.5 %all-gather.11.cloned.1.call-start = ((), (), s32[]{:S(2)}) async-start(), calls=%async_computation.4 | async-start | bytes 1179648 | tf_op jit(solution)/shard_map/while/body/eval_jaxpr/all_gather | solution.py:122
  264.1 60.8 %all-to-all-start = ((bf16[64,8,2048]{2,1,0:T(8,128)(2,1)}), bf16[64,8,2048]{2,1,0:T(8,128)(2,1)}, u32[]{:S(2)}, u32[]{:S(2)}) async-start(bf16[64,8,2048]{2,1,0:T(8,128)(2,1)} %bitcast.287), calls=%async_computation | async-start | bytes 4194304 | tf_op jit(solution)/shard_map/while/body/eval_jaxpr/all_to_all | solution.py:175
  270.2 140.2 %all-gather.9.cloned.1.call-start = ((), (), s32[]{:S(2)}) async-start(), calls=%async_computation.3 | async-start | bytes 2359296 | tf_op jit(solution)/shard_map/while/body/eval_jaxpr/all_gather | solution.py:118
  325.0 6.0 copy-start.10
  334.4 88.5 %all-to-all-start.1 = ((bf16[64,8,2048]{2,1,0:T(8,128)(2,1)}), bf16[64,8,2048]{2,1,0:T(8,128)(2,1)S(1)}, u32[]{:S(2)}, u32[]{:S(2)}) async-start(bf16[64,8,2048]{2,1,0:T(8,128)(2,1)} %fusion.196), calls=%async_computation.1 | async-start | bytes 4194304 | tf_op jit(solution)/shard_map/while/body/eval_jaxpr/all_to_all | solution.py:180
  347.7 101.2 %reduce-scatter.2.cloned.1.call-start = ((), (), s32[]{:S(2)}) async-start(), calls=%async_computation.5 | async-start | bytes 589824 | tf_op jit(solution)/shard_map/while/body/eval_jaxpr/reduce_scatter | solution.py:138
  450.5 6.1 collective-permute-start
  456.6 82.7 %all-gather.11.cloned.1.call-start = ((), (), s32[]{:S(2)}) async-start(), calls=%async_computation.4 | async-start | bytes 1179648 | tf_op jit(solution)/shard_map/while/body/eval_jaxpr/all_gather | solution.py:122
  482.3 61.0 %all-to-all-start = ((bf16[64,8,2048]{2,1,0:T(8,128)(2,1)}), bf16[64,8,2048]{2,1,0:T(8,128)(2,1)}, u32[]{:S(2)}, u32[]{:S(2)}) async-start(bf16[64,8,2048]{2,1,0:T(8,128)(2,1)} %bitcast.287), calls=%async_computation | async-start | bytes 4194304 | tf_op jit(solution)/shard_map/while/body/eval_jaxpr/all_to_all | solution.py:175
  488.6 136.0 %all-gather.9.cloned.1.call-start = ((), (), s32[]{:S(2)}) async-start(), calls=%async_computation.3 | async-start | bytes 2359296 | tf_op jit(solution)/shard_map/while/body/eval_jaxpr/all_gather | solution.py:118
  543.4 6.0 copy-start.10
  552.8 84.3 %all-to-all-start.1 = ((bf16[64,8,2048]{2,1,0:T(8,128)(2,1)}), bf16[64,8,2048]{2,1,0:T(8,128)(2,1)S(1)}, u32[]{:S(2)}, u32[]{:S(2)}) async-start(bf16[64,8,2048]{2,1,0:T(8,128)(2,1)} %fusion.196), calls=%async_computation.1 | async-start | bytes 4194304 | tf_op jit(solution)/shard_map/while/body/eval_jaxpr/all_to_all | solution.py:180
  566.1 103.3 %reduce-scatter.2.cloned.1.call-start = ((), (), s32[]{:S(2)}) async-start(), calls=%async_computation.5 | async-start | bytes 589824 | tf_op jit(solution)/shard_map/while/body/eval_jaxpr/reduce_scatter | solution.py:138
  670.9 6.1 collective-permute-start
  677.9 6.5 collective-permute-start.1
  (6 other events, 9.1 us)
Sparse Core Ops, SparseCore 0:
  39.6 60.0 all-gather.10
  101.3 83.3 all-gather.8
  197.3 33.3 reduce-scatter.1
  260.8 59.9 all-gather.10
  322.3 88.0 all-gather.8
  423.0 25.9 reduce-scatter.1
  479.0 60.1 all-gather.10
  540.8 83.6 all-gather.8
  637.1 32.1 reduce-scatter.1
where the time goes:
time: 698 us; the launch traced here: 692 us
  waiting for transfers between devices  381 us (55%)
  matrix products  78.5 us (11%)
  starting transfers between devices  77.1 us (11%)
  local copies, waits for them, and re-layouts  62.5 us (9%)
  blocking collectives  49.2 us (7%)
  other arithmetic  26 us (4%)
  between operations  13.2 us (2%)
    all_gather x3, waiting for transfers between devices, attention_block(): piece = lax.all_gather(cache_rows, 'seq', axis=0, tiled=True)  179 us
    all_gather x3, waiting for transfers between devices, attention_block(): piece = lax.all_gather(fresh, 'seq', axis=0, tiled=True)  105 us
    reduce_scatter x3, waiting for transfers between devices, attention_block(): lax.psum_scatter(jnp.dot(spread, out_flat, preferred_element_type=jnp.flo...  87.7 us
    all_gather x3, blocking collectives, attention_block(): gathered = lax.all_gather(own_rows, 'expert', axis=0, tiled=True)  49.2 us
    all_to_all x3, starting transfers between devices, expert_block(): lax.all_to_all(partial_value, ('seq', 'expert'), split_axis=0, concat_axi...  40.2 us
    all_to_all x3, starting transfers between devices, expert_block(): lax.all_to_all(copies, ('seq', 'expert'), split_axis=0, concat_axis=0, ti...  20.8 us
    dot_general x3, matrix products, expert_hidden(): jnp.dot(rows, single.reshape(single.shape[0], -1), preferred_element_type...  18.1 us
    ppermute x4, starting transfers between devices, passed_along(): lax.ppermute(value, axis, [(source, source + steps) for source in range(i...  15.7 us
  transfers between devices with their start and end apart: 19, of which 13 were waited for; matrix products, arithmetic and copies ran while one was open for 19% of the time, Pallas kernels for 0%

commit v1 on v0

--- a/solution.py
+++ b/solution.py
@@ -9,12 +9,6 @@
 EPS = 1e-06
 THETA = 10000.0
 NEGATIVE = -1e30
-
-
-def passed_along(value, axis, steps):
-    count = lax.axis_size(axis)
-    initial, last = (max(0, -steps), min(count, count - steps))
-    return lax.ppermute(value, axis, [(source, source + steps) for source in range(initial, last)])
 
 
 def rms_scale(values, gain):
@@ -207,48 +201,23 @@
     in_weight,
     down_weight,
 ):
-    batches = tokens.shape[0]
-    half_count = batches // 2
-    section = lax.axis_index("section")
-
-    def attend(batch):
-        return attention_block(
-            select_batch(tokens, batch),
-            select_batch(prompt_lengths, batch),
-            select_batch(cache_lengths, batch),
-            select_batch(kv_cache, batch),
-            select_batch(attn_routes, batch),
-            attn_gain,
-            attn_mix,
-            query_weight,
-            kv_weight,
-            out_weight,
-        )
-
-    def finish(middle, batch):
-        return expert_block(
-            middle, select_batch(ffn_routes, batch), ffn_gain, ffn_mix, in_weight, down_weight
-        )
-
-    blank = jnp.zeros(tokens.shape[1:], jnp.bfloat16)
-    first_section = section == 0
-
-    def one_tick(incoming, tick):
-        ahead = jnp.minimum(tick, batches - 1)
-        behind = jnp.maximum(tick - 1, 0)
-        attended_rows = attend(ahead)
-        finished_rows = finish(incoming, behind)
-        produced = jnp.where(first_section, attended_rows, finished_rows)
-        passed = passed_along(produced, "section", 1)
-        return (passed, produced)
-
-    ticks = jnp.arange(batches + 1, dtype=jnp.int32)
-    _, produced_all = lax.scan(one_tick, blank, ticks)
-    finished = produced_all[1:]
-    former_half = finished[:half_count]
-    latter_half = finished[half_count:]
-    returned = passed_along(former_half, "section", -1)
-    return jnp.where(first_section, returned, latter_half)
+    batch = lax.axis_index("section")
+    middle = attention_block(
+        select_batch(tokens, batch),
+        select_batch(prompt_lengths, batch),
+        select_batch(cache_lengths, batch),
+        select_batch(kv_cache, batch),
+        select_batch(attn_routes, batch),
+        attn_gain,
+        attn_mix,
+        query_weight,
+        kv_weight,
+        out_weight,
+    )
+    finished = expert_block(
+        middle, select_batch(ffn_routes, batch), ffn_gain, ffn_mix, in_weight, down_weight
+    )
+    return finished[None]
 
 
 def solution(mesh):

time: 698 us -> 284 us (0.41)
  waiting for transfers between devices: 381 us -> 123 us
  starting transfers between devices: 77.1 us -> 5.34 us
  matrix products: 78.5 us -> 25.3 us
  local copies, waits for them, and re-layouts: 62.5 us -> 44.3 us
  other arithmetic: 26 us -> 18.4 us
    all_gather x3 -> x1, waiting for transfers between devices: 179 us -> 60 us  [attention_block(): piece = lax.all_gather(cache_rows, 'seq', axis=0, tiled=True)]
    all_gather x3 -> x1, waiting for transfers between devices: 105 us -> 5.47 us  [attention_block(): piece = lax.all_gather(fresh, 'seq', axis=0, tiled=True)]
    reduce_scatter x3 -> x1, waiting for transfers between devices: 87.7 us -> 30.2 us  [attention_block(): lax.psum_scatter(jnp.dot(spread, out_flat, preferred_element_type=jnp.flo...]
    all_to_all x0 -> x1, blocking collectives: none -> 38.1 us  [expert_block(): lax.all_to_all(copies, ('seq', 'expert'), split_axis=0, concat_axis=0, ti...]
    all_to_all x3 -> x1, starting transfers between devices: 40.2 us -> 5.26 us  [expert_block(): lax.all_to_all(partial_value, ('seq', 'expert'), split_axis=0, concat_axi...]
    all_gather x3 -> x1, blocking collectives: 49.2 us -> 15 us  [attention_block(): gathered = lax.all_gather(own_rows, 'expert', axis=0, tiled=True)]
    all_to_all x3 -> x1, waiting for transfers between devices: 0.01 us -> 27.5 us  [expert_block(): lax.all_to_all(partial_value, ('seq', 'expert'), split_axis=0, concat_axi...]
    all_to_all x3 -> x0, starting transfers between devices: 20.8 us -> none  [expert_block(): lax.all_to_all(copies, ('seq', 'expert'), split_axis=0, concat_axis=0, ti...]
  transfers between devices with their start and end apart: 19 -> 4, of which waited for: 13 -> 4; matrix products, arithmetic and copies ran while one was open for 19% -> 14% of each run, Pallas kernels for 0% -> 0%
where the time goes in v1:
time: 284 us; the launch traced here: 283 us
  waiting for transfers between devices  123 us (43%)
  blocking collectives  53 us (19%)
  local copies, waits for them, and re-layouts  44.3 us (16%)
  matrix products  25.3 us (9%)
  other arithmetic  18.4 us (6%)
  between operations  13.6 us (5%)
  starting transfers between devices  5.34 us (2%)
    all_gather x1, waiting for transfers between devices, attention_block(): piece = lax.all_gather(cache_rows, 'seq', axis=0, tiled=True)  60 us
    all_to_all x1, blocking collectives, expert_block(): lax.all_to_all(copies, ('seq', 'expert'), split_axis=0, concat_axis=0, ti...  38.1 us
    reduce_scatter x1, waiting for transfers between devices, attention_block(): lax.psum_scatter(jnp.dot(spread, out_flat, preferred_element_type=jnp.flo...  30.2 us
    all_to_all x1, waiting for transfers between devices, expert_block(): lax.all_to_all(partial_value, ('seq', 'expert'), split_axis=0, concat_axi...  27.5 us
    all_gather x1, blocking collectives, attention_block(): gathered = lax.all_gather(own_rows, 'expert', axis=0, tiled=True)  15 us
    unnamed x57, local copies, waits for them, and re-layouts  11.2 us
    dot_general x2, local copies, waits for them, and re-layouts, attention_block(): jnp.dot(normed, query_weight.reshape(query_weight.shape[0], -1), preferre...  6.91 us
  transfers between devices with their start and end apart: 4, of which 4 were waited for; matrix products, arithmetic and copies ran while one was open for 14% of the time, Pallas kernels for 0%

profile of v1, /device:TPU:1, one launch (start us, length us, event | category | flops | bytes accessed | tf_op | source)
XLA Modules:
  0.0 283.1 jit_solution(11401811092933586299)
XLA Ops:
  8.2 15.0 %all-gather = bf16[1,128,2048]{2,1,0:T(8,128)(2,1)S(1)} all-gather(bf16[1,16,2048]{2,1,0:T(8,128)(2,1)S(1)} %constant_dynamic-slice_fusion.5), channel_id=2, replica_groups=mesh['section'=2,'seq'=8,'expert'=8] {'expert'}, dimensions={1}, use_global_device_ids=true | all-gather | bytes 589824 | tf_op jit(solution)/shard_map/all_gather | solution.py:62
  23.3 3.4 %copy.115 = bf16[256,8,2,256]{3,1,2,0:T(8,128)(2,1)} copy(bf16[256,8,2,256]{3,2,1,0:T(2,128)(2,1)} %bitcast.189) | data formatting | bytes 4194304
  26.7 4.0 %copy.97 = bf16[512,2048]{1,0:T(8,128)(2,1)} copy(bf16[512,2048]{0,1:T(8,128)(2,1)} %bitcast.186) | data formatting | bytes 4194304 | tf_op jit(solution)/shard_map/dot_general | solution.py:78
  30.7 2.4 fusion.42
  35.2 1.3 fusion.81
  39.4 1.5 pad_maximum_fusion.1
  41.0 1.8 constant_dynamic-slice_fusion.1
  42.8 1.8 copy.113
  44.7 1.5 copy.92
  46.2 1.5 copy.93
  48.3 2.4 gather_fusion.1
  51.0 5.2 %copy.114 = bf16[256,8,4,256]{3,1,2,0:T(8,128)(2,1)} copy(bf16[256,8,4,256]{3,2,1,0:T(4,128)(2,1)} %bitcast.187) | data formatting | bytes 8388608
  56.2 6.5 %copy.89 = bf16[1024,2048]{1,0:T(8,128)(2,1)} copy(bf16[1024,2048]{0,1:T(8,128)(2,1)} %bitcast.183) | data formatting | bytes 8388608 | tf_op jit(solution)/shard_map/dot_general | solution.py:71
  62.7 3.7 %fusion.44 = f32[128,4,2,128]{3,0,2,1:T(8,128)S(1)} fusion(bf16[4,2,128,2048]{3,2,1,0:T(8,128)(2,1)} %bitcast.182, bf16[1,128,2048]{2,1,0:T(8,128)(2,1)S(1)} %all-gather, f32[2048]{0:T(1024)S(1)} %copy-done.12, f32[128]{0:T(128)S(1)} %copy-done.23), kind=kOutput, calls=%fused_computation.52 | convolution fusion | flops 537919488 | bytes 5251584 | tf_op jit(solution)/shard_map/dot_general | solution.py:71
  66.9 1.9 gather_fusion.2
  73.4 2.0 subtract_convert_fusion
  75.7 5.5 %all-gather.5.cloned.1.call-done = bf16[1024,2,256]{0,2,1:T(8,128)(2,1)} async-done(((bf16[128,2,256]{0,2,1:T(8,128)(2,1)}), bf16[1024,2,256]{0,2,1:T(8,128)(2,1)}) %all-gather.5.cloned.1.call-update) | async-done | bytes 1048592 | tf_op jit(solution)/shard_map/all_gather | solution.py:116
  81.2 2.1 fusion.105
  83.3 2.0 fusion.15
  85.3 60.0 %all-gather.7.cloned.1.call-done = bf16[1,2048,2,256]{1,3,2,0:T(8,128)(2,1)} async-done(((bf16[1,256,2,256]{1,3,2,0:T(8,128)(2,1)}), bf16[1,2048,2,256]{1,3,2,0:T(8,128)(2,1)}) %all-gather.7.cloned.1.call-update) | async-done | bytes 2097168 | tf_op jit(solution)/shard_map/all_gather | solution.py:112
  145.3 1.8 fusion.104
  148.3 1.4 fusion.3
  150.7 1.4 fusion.27
  154.0 3.7 %fusion.9 = bf16[128,2048]{1,0:T(8,128)(2,1)} fusion(bf16[4,256,2048]{2,1,0:T(8,128)(2,1)} %param.26, bf16[128,4,256]{2,1,0:T(4,128)(2,1)S(1)} %convolution_convert_fusion.2), kind=kOutput, calls=%fused_computation.16 | convolution fusion | flops 537133056 | bytes 4980736 | tf_op jit(solution)/shard_map/dot_general | solution.py:133
  158.7 30.2 %reduce-scatter.2.cloned.1.call-done = bf16[16,2048]{1,0:T(8,128)(2,1)} async-done(((bf16[128,2048]{1,0:T(8,128)(2,1)}), bf16[16,2048]{1,0:T(8,128)(2,1)}) %reduce-scatter.2.cloned.1.call-update) | async-done | bytes 65552 | tf_op jit(solution)/shard_map/reduce_scatter | solution.py:132
  190.4 38.1 %all_to_all.10 = bf16[64,8,2048]{2,1,0:T(8,128)(2,1)S(1)} all-to-all(bf16[64,8,2048]{2,1,0:T(8,128)(2,1)S(1)} %bitcast.185), channel_id=1, replica_groups=mesh['section'=2,'seq'=8,'expert'=8] {'seq','expert'}, dimensions={0} | all-to-all | bytes 4194304 | tf_op jit(solution)/shard_map/all_to_all | solution.py:169
  228.5 5.2 %fusion = f32[512,2,704]{0,2,1:T(8,128)S(1)} fusion(bf16[1,2048,2,704]{1,3,2,0:T(8,128)(2,1)} %param.28, bf16[64,8,2048]{2,1,0:T(8,128)(2,1)S(1)} %all_to_all.10), kind=kOutput, calls=%fused_computation.4 | convolution fusion | flops 2952790016 | bytes 10747904 | tf_op jit(solution)/shard_map/dot_general | solution.py:143
  233.7 3.3 %fusion.6 = bf16[64,8,2048]{2,1,0:T(8,128)(2,1)} fusion(bf16[1,704,2048]{2,1,0:T(8,128)(2,1)S(1)} %copy-done, f32[512,2,704]{0,2,1:T(8,128)S(1)} %fusion), kind=kOutput, calls=%fused_computation.14 | convolution fusion | flops 1479606272 | bytes 7864320 | tf_op jit(solution)/shard_map/dot_general | solution.py:172
  237.0 5.3 %all-to-all-start.1 = ((bf16[64,8,2048]{2,1,0:T(8,128)(2,1)}), bf16[64,8,2048]{2,1,0:T(8,128)(2,1)}, u32[]{:S(2)}, u32[]{:S(2)}) async-start(bf16[64,8,2048]{2,1,0:T(8,128)(2,1)} %fusion.6), calls=%async_computation.2 | async-start | bytes 4194304 | tf_op jit(solution)/shard_map/all_to_all | solution.py:174
  243.8 27.5 %all-to-all-done.1 = bf16[64,8,2048]{2,1,0:T(8,128)(2,1)} async-done(((bf16[64,8,2048]{2,1,0:T(8,128)(2,1)}), bf16[64,8,2048]{2,1,0:T(8,128)(2,1)}, u32[]{:S(2)}, u32[]{:S(2)}) %all-to-all-start.1) | async-done | bytes 2097184 | tf_op jit(solution)/shard_map/all_to_all | solution.py:174
  271.2 2.0 convert_reduce_fusion
  273.3 1.3 gather_fusion
  (136 shorter events, 23.1 us)
Async XLA Ops:
  6.5 227.2 %copy-start = (bf16[1,704,2048]{2,1,0:T(8,128)(2,1)S(1)}, bf16[1,704,2048]{2,1,0:T(8,128)(2,1)}, u32[]{:S(2)}) copy-start(bf16[1,704,2048]{2,1,0:T(8,128)(2,1)} %param.29) | copy-start | bytes 8650756
  6.5 74.7 %all-gather.5.cloned.1.call-start = ((), (), s32[]{:S(2)}) async-start(), calls=%async_computation.3 | async-start | bytes 1179648 | tf_op jit(solution)/shard_map/all_gather | solution.py:116
  23.3 7.4 %copy-start.22 = (f32[128]{0:T(128)}, f32[128]{0:T(128)S(1)}, u32[]{:S(2)}) copy-start(f32[128]{0:T(128)S(1)} %add_rsqrt_fusion.1) | copy-start | bytes 1540
  26.7 4.0 %copy-start.12 = (f32[2048]{0:T(1024)S(1)}, f32[2048]{0:T(1024)}, u32[]{:S(2)}) copy-start(f32[2048]{0:T(1024)} %param.21) | copy-start | bytes 24580
  30.7 3.1 %copy-start.17 = (s32[2,3]{1,0:T(2,128)S(1)}, s32[2,3]{1,0:T(2,128)}, u32[]{:S(2)}) copy-start(s32[2,3]{1,0:T(2,128)} %param.16) | copy-start | bytes 76
  30.7 3.1 %copy-start.24 = (s32[2,3]{1,0:T(2,128)S(1)}, s32[2,3]{1,0:T(2,128)}, u32[]{:S(2)}) copy-start(s32[2,3]{1,0:T(2,128)} %param.17) | copy-start | bytes 76
  33.1 14.6 %copy-start.14 = (s32[2,128,2]{1,2,0:T(2,128)S(1)}, s32[2,128,2]{1,2,0:T(2,128)}, u32[]{:S(2)}) copy-start(s32[2,128,2]{1,2,0:T(2,128)} %param.19) | copy-start | bytes 6148
  35.2 1.3 copy-start.15
  36.5 0.8 copy-start.18
  38.8 0.6 copy-start.7
  38.8 0.6 copy-start.8
  39.4 8.5 %copy-start.23 = (f32[128]{0:T(128)S(1)}, f32[128]{0:T(128)}, u32[]{:S(2)}) copy-start(f32[128]{0:T(128)} %copy-done.22) | copy-start | bytes 1540
  39.4 8.6 %copy-start.26 = (bf16[2048,4]{0,1:T(4,128)(2,1)S(1)}, bf16[2048,4]{0,1:T(4,128)(2,1)}, u32[]{:S(2)}) copy-start(bf16[2048,4]{0,1:T(4,128)(2,1)} %param.23) | copy-start | bytes 49156
  41.0 104.3 %all-gather.7.cloned.1.call-start = ((), (), s32[]{:S(2)}) async-start(), calls=%async_computation.5 | async-start | bytes 2359296 | tf_op jit(solution)/shard_map/all_gather | solution.py:112
  44.7 144.2 %reduce-scatter.2.cloned.1.call-start = ((), (), s32[]{:S(2)}) async-start(), calls=%async_computation.4 | async-start | bytes 589824 | tf_op jit(solution)/shard_map/reduce_scatter | solution.py:132
  62.7 6.3 %copy-start.19 = (s32[128]{0:T(128)S(1)}, s32[128]{0:T(128)}, u32[]{:S(2)}) copy-start(s32[128]{0:T(128)} %copy-done.18) | copy-start | bytes 1540
  62.7 6.6 %copy-start.21 = (s32[3,1]{0,1:T(1,128)S(1)}, s32[3,1]{0,1:T(1,128)}, u32[]{:S(2)}) copy-start(s32[3,1]{0,1:T(1,128)} %get-tuple-element.33) | copy-start | bytes 40
  62.7 8.2 %copy-start.16 = (s32[3,1]{0,1:T(1,128)S(1)}, s32[3,1]{0,1:T(1,128)}, u32[]{:S(2)}) copy-start(s32[3,1]{0,1:T(1,128)} %copy-done.15) | copy-start | bytes 40
  81.2 2.1 copy-start.2
  81.2 2.1 copy-start.4
  145.3 1.8 copy-start.5
  148.3 1.6 copy-start.1
  148.3 1.6 copy-start.3
  150.7 1.4 copy-start.6
  152.2 1.1 copy-start.10
  152.2 1.1 copy-start.11
  153.9 3.8 %copy-start.20 = (s32[2,16,2]{1,2,0:T(2,128)S(1)}, s32[2,16,2]{1,2,0:T(2,128)}, u32[]{:S(2)}) copy-start(s32[2,16,2]{1,2,0:T(2,128)} %param.20) | copy-start | bytes 772
  153.9 34.9 %copy-start.9 = (bf16[2,16,2048]{2,1,0:T(8,128)(2,1)S(1)}, bf16[2,16,2048]{2,1,0:T(8,128)(2,1)}, u32[]{:S(2)}) copy-start(bf16[2,16,2048]{2,1,0:T(8,128)(2,1)} %param.15) | copy-start | bytes 393220
  153.9 35.9 %copy-start.13 = (f32[2048]{0:T(1024)S(1)}, f32[2048]{0:T(1024)}, u32[]{:S(2)}) copy-start(f32[2048]{0:T(1024)} %param.22) | copy-start | bytes 24580
  237.0 5.7 %copy-start.25 = (bf16[2048,8]{0,1:T(8,128)(2,1)S(1)}, bf16[2048,8]{0,1:T(8,128)(2,1)}, u32[]{:S(2)}) copy-start(bf16[2048,8]{0,1:T(8,128)(2,1)} %param.27) | copy-start | bytes 98308
  237.0 34.2 %all-to-all-start.1 = ((bf16[64,8,2048]{2,1,0:T(8,128)(2,1)}), bf16[64,8,2048]{2,1,0:T(8,128)(2,1)}, u32[]{:S(2)}, u32[]{:S(2)}) async-start(bf16[64,8,2048]{2,1,0:T(8,128)(2,1)} %fusion.6), calls=%async_computation.2 | async-start | bytes 4194304 | tf_op jit(solution)/shard_map/all_to_all | solution.py:174
Sparse Core Ops, SparseCore 0:
  41.1 40.0 all-gather.4
  82.8 62.4 all-gather.6
  157.8 31.0 reduce-scatter.1

commit v2 on v1

v2 whole, which is shorter than its diff:
```python
import math

import jax
import jax.numpy as jnp
from jax import lax
from jax.experimental import pallas as pl
from jax.experimental.pallas import tpu as pltpu
from jax.sharding import PartitionSpec as P

HEAD_DIM = 128


EPS = 1e-06
THETA = 10000.0
NEGATIVE = -1e30


def rms_scale(values, gain):
    widened = values.astype(jnp.float32)
    inverse = lax.rsqrt(jnp.mean(widened * widened, axis=-1, keepdims=True) + EPS)
    return (widened * inverse * gain).astype(jnp.bfloat16)


def route_gates(normed, mixing, routes):
    logits = jnp.dot(normed, mixing, preferred_element_type=jnp.float32)
    chosen = jnp.take_along_axis(logits, routes, axis=1)
    leading = jax.nn.sigmoid(chosen[:, 0] - chosen[:, 1])
    return jnp.stack([leading, 1.0 - leading], axis=1)


def select_batch(values, batch):
    return lax.dynamic_index_in_dim(values, batch, 0, keepdims=False)


MESH_ID = pl.DeviceIdType.MESH
NT = (((1,), (1,)), ((), ()))


def send(src, dst, sends, recvs, index, device):
    return pltpu.make_async_remote_copy(
        src_ref=src,
        dst_ref=dst,
        send_sem=sends.at[index],
        recv_sem=recvs.at[index],
        device_id=device,
        device_id_type=MESH_ID,
    )


def iota(shape, dim):
    return lax.broadcasted_iota(jnp.int32, shape, dim)


def untangle(groups):
    per = 256 // groups
    row, column = iota((256, 256), 0), iota((256, 256), 1)
    source = lax.rem(row, per) * groups + row // per
    return (column == source).astype(jnp.bfloat16)


def as_column(line, count):
    square = jnp.broadcast_to(line, (count, count))
    kept = jnp.where(iota((count, count), 0) == iota((count, count), 1), square, 0.0)
    return jnp.sum(kept, axis=1, keepdims=True)


class Spread:
    def __init__(self, buffer, sends, recvs, section, seq, expert):
        self.buffer, self.sends, self.recvs = buffer, sends, recvs
        self.near = seq
        self.right = lax.rem(seq + 2, 8)
        self.left = lax.rem(seq + 6, 8)
        self.across = seq + 1 - 2 * lax.rem(seq, 2)
        self.place = lambda other: (section, other, expert)
        right_across = lax.rem(self.across + 2, 8)
        self.copies = [
            self.copy(seq, self.across, 0),
            self.copy(seq, self.right, 1),
            self.copy(seq, self.left, 2),
            self.copy(self.across, self.right, 3),
            self.copy(self.across, self.left, 4),
            self.copy(self.left, self.right, 5),
            self.copy(right_across, self.left, 6),
        ]

    def copy(self, block, target, index):
        ref = self.buffer.at[block]
        return send(ref, ref, self.sends, self.recvs, index, self.place(target))

    def first(self):
        for index in (1, 2, 0):
            self.copies[index].start()

    def second(self):
        self.copies[0].wait_recv()
        self.copies[3].start()
        self.copies[4].start()

    def third(self):
        self.copies[1].wait_recv()
        self.copies[5].start()
        self.copies[4].wait_recv()
        self.copies[6].start()

    def finish(self):
        for index in (2, 3, 5, 6):
            self.copies[index].wait_recv()

    def drain(self):
        for index in range(7):
            self.copies[index].wait_send()


def attention_kernel(
    lengths_ref,
    cached_ref,
    tokens_ref,
    routes_ref,
    gain_ref,
    mix_ref,
    cache_hbm,
    query_hbm,
    kv_hbm,
    out_hbm,
    middle_ref,
    raw_cache,
    raw_query,
    raw_kv,
    weights,
    out_weights,
    normed,
    projected,
    cache_all,
    fresh_all,
    queries,
    top,
    total,
    summed,
    partial,
    arrived,
    load_sems,
    token_sends,
    token_recvs,
    cache_sends,
    cache_recvs,
    fresh_sends,
    fresh_recvs,
    part_sends,
    part_recvs,
):
    section = lax.axis_index("section")
    seq = lax.axis_index("seq")
    expert = lax.axis_index("expert")
    own_x = seq // 2
    loads = [
        pltpu.make_async_copy(cache_hbm.at[section], raw_cache, load_sems.at[0]),
        pltpu.make_async_copy(kv_hbm, raw_kv, load_sems.at[1]),
        pltpu.make_async_copy(query_hbm, raw_query, load_sems.at[2]),
        pltpu.make_async_copy(out_hbm, out_weights, load_sems.at[3]),
    ]
    for load in loads:
        load.start()

    caches = Spread(cache_all, cache_sends, cache_recvs, section, seq, expert)
    freshes = Spread(fresh_all, fresh_sends, fresh_recvs, section, seq, expert)
    barrier = pltpu.get_barrier_semaphore()
    for other in (caches.right, caches.left, caches.across):
        pl.semaphore_signal(
            barrier, inc=1, device_id=(section, other, expert), device_id_type=MESH_ID
        )
    for step in range(1, 8):
        peer = lax.rem(expert + step, 8)
        pl.semaphore_signal(barrier, inc=1, device_id=(section, seq, peer), device_id_type=MESH_ID)

    rows = tokens_ref[section].astype(jnp.float32)
    inverse = lax.rsqrt(jnp.mean(rows * rows, axis=-1, keepdims=True) + EPS)
    own_rows = pl.ds(pl.multiple_of(expert * 16, 16), 16)
    normed[own_rows, :] = (rows * inverse * gain_ref[...]).astype(jnp.bfloat16)
    pl.semaphore_wait(barrier, 10)
    token_copies = []
    for step in range(1, 8):
        peer = lax.rem(expert + step, 8)
        ref = normed.at[own_rows, :]
        copy = send(ref, ref, token_sends, token_recvs, step - 1, (section, seq, peer))
        copy.start()
        token_copies.append(copy)

    by_head = untangle(4)
    order = (0, 2, 1, 3)
    loads[0].wait()
    for step in range(4):
        block = jnp.dot(
            by_head, raw_cache[pl.ds(step * 256, 256), :], preferred_element_type=jnp.float32
        ).astype(jnp.bfloat16)
        for group in range(4):
            cache_all[seq, order[group], pl.ds(step * 64, 64), :] = block[
                group * 64 : group * 64 + 64, :
            ]
    caches.first()

    loads[1].wait()

    def kv_step(step, carried):
        base = pl.multiple_of(step * 512, 512)
        pair = jnp.concatenate(
            [raw_kv[pl.ds(base, 256), :], raw_kv[pl.ds(base + 256, 256), :]], axis=1
        )
        block = jnp.dot(by_head, pair, preferred_element_type=jnp.float32).astype(jnp.bfloat16)
        for half in range(2):
            at = pl.ds(pl.multiple_of(step * 128 + half * 64, 64), 64)
            for group in range(4):
                column = 1024 + order[group] * 128
                weights[at, column : column + 128] = block[
                    group * 64 : group * 64 + 64, half * 128 : half * 128 + 128
                ]
        return carried

    lax.fori_loop(0, 16, kv_step, 0)
    by_expert = untangle(8)
    loads[2].wait()

    def query_step(step, carried):
        base = pl.multiple_of(step * 512, 512)
        pair = jnp.concatenate(
            [raw_query[pl.ds(base, 256), :], raw_query[pl.ds(base + 256, 256), :]], axis=1
        )
        block = jnp.dot(by_expert, pair, preferred_element_type=jnp.float32).astype(jnp.bfloat16)
        for half in range(2):
            at = pl.ds(pl.multiple_of(step * 64 + half * 32, 32), 32)
            for group in range(8):
                column = (group % 4) * 256 + (group // 4) * 128
                weights[at, column : column + 128] = block[
                    group * 32 : group * 32 + 32, half * 128 : half * 128 + 128
                ]
        return carried

    lax.fori_loop(0, 32, query_step, 0)

    end_0 = lengths_ref[section, 0]
    end_1 = end_0 + lengths_ref[section, 1]
    held_0, held_1, held_2 = (cached_ref[section, prompt] for prompt in range(3))
    index = seq * 128 + iota((128, 1), 0)
    in_1, in_2 = index >= end_0, index >= end_1
    segment = in_1.astype(jnp.int32) + in_2.astype(jnp.int32)
    shift = jnp.where(in_2, held_2 - end_1, jnp.where(in_1, held_1 - end_0, held_0))
    place = (shift + index).astype(jnp.float32)
    lane = iota((1, 128), 1)
    freq = jnp.exp(lax.rem(lane, 64).astype(jnp.float32) * (-math.log(THETA) / 64))
    angle = place * freq
    cosine = jnp.cos(angle)
    sine = jnp.where(lane < 64, -1.0, 1.0) * jnp.sin(angle)

    def rope(value):
        return value * cosine + pltpu.roll(value, 64, 1) * sine

    routes = routes_ref[section].astype(jnp.float32)
    route_0 = as_column(routes[0:1, :], 128)
    route_1 = as_column(routes[1:2, :], 128)

    for copy in token_copies:
        copy.wait_recv()
    caches.second()

    def project(tile, carried):
        at = pl.ds(pl.multiple_of(tile * 256, 256), 256)
        projected[:, at] = jnp.dot(
            normed[...], weights[:, at], preferred_element_type=jnp.float32
        )
        return carried

    lax.fori_loop(4, 6, project, 0)
    for head in range(2):
        keys = projected[:, 1024 + head * 128 : 1152 + head * 128]
        fresh_all[seq, head, :, :] = rope(keys).astype(jnp.bfloat16)
        values = projected[:, 1280 + head * 128 : 1408 + head * 128]
        fresh_all[seq, 2 + head, :, :] = values.astype(jnp.bfloat16)
    freshes.first()
    lax.fori_loop(0, 4, project, 0)
    caches.third()

    logits = lax.dot_general(normed[...], mix_ref[...], NT, preferred_element_type=jnp.float32)

    def chosen_logit(route):
        chosen = jnp.where(route == 0.0, logits[:, 0:1], 0.0)
        for one in range(1, 4):
            chosen = chosen + jnp.where(route == float(one), logits[:, one : one + 1], 0.0)
        return chosen

    gate_0 = jax.nn.sigmoid(chosen_logit(route_0) - chosen_logit(route_1))
    gate_1 = 1.0 - gate_0

    for head in range(2):
        for place_of, route in ((0, route_0), (1, route_1)):
            query = jnp.zeros((128, 128), jnp.float32)
            for one in range(4):
                column = one * 256 + head * 128
                query = jnp.where(
                    route == float(one), projected[:, column : column + 128], query
                )
            queries[head, pl.ds(place_of * 128, 128), :] = rope(query).astype(jnp.bfloat16)

    top[...] = jnp.full_like(top, NEGATIVE)
    total[...] = jnp.zeros_like(total)
    summed[...] = jnp.zeros_like(summed)
    query_segment = jnp.concatenate([segment, segment], axis=0)
    query_index = jnp.concatenate([index, index], axis=0)
    scale = HEAD_DIM ** (-0.5)
    cache_1 = held_0
    cache_2 = held_0 + held_1

    def absorb(head, keys, values, allowed):
        scores = (
            lax.dot_general(queries[head], keys, NT, preferred_element_type=jnp.float32) * scale
        )
        scores = jnp.where(allowed, scores, NEGATIVE)
        old = top[head]
        new = jnp.maximum(old, jnp.max(scores, axis=1, keepdims=True))
        share = jnp.exp(scores - new[:, 0:1])
        shrink = jnp.exp(old - new)
        total[head] = total[head] * shrink + jnp.sum(share, axis=1, keepdims=True)
        summed[head] = summed[head] * shrink + jnp.dot(
            share.astype(jnp.bfloat16), values, preferred_element_type=jnp.float32
        )
        top[head] = new

    def cache_chunk(step, carried):
        first = lax.rem(own_x + step, 4) * 2
        slot = first * 256 + iota((1, 512), 1)
        key_segment = (slot >= cache_1).astype(jnp.int32) + (slot >= cache_2).astype(jnp.int32)
        allowed = query_segment == key_segment
        for head in range(2):
            keys = jnp.concatenate([cache_all[first, head], cache_all[first + 1, head]], axis=0)
            values = jnp.concatenate(
                [cache_all[first, 2 + head], cache_all[first + 1, 2 + head]], axis=0
            )
            absorb(head, keys, values, allowed)
        return carried

    def fresh_chunk(step, carried):
        first = lax.rem(own_x + step, 4) * 2
        slot = first * 128 + iota((1, 256), 1)
        key_segment = (slot >= end_0).astype(jnp.int32) + (slot >= end_1).astype(jnp.int32)
        allowed = (query_segment == key_segment) & (slot <= query_index)
        for head in range(2):
            keys = jnp.concatenate([fresh_all[first, head], fresh_all[first + 1, head]], axis=0)
            values = jnp.concatenate(
                [fresh_all[first, 2 + head], fresh_all[first + 1, 2 + head]], axis=0
            )
            absorb(head, keys, values, allowed)
        return carried

    freshes.second()
    cache_chunk(0, 0)
    caches.finish()
    freshes.third()
    lax.fori_loop(1, 4, cache_chunk, 0)
    freshes.finish()
    lax.fori_loop(0, 4, fresh_chunk, 0)

    pieces = []
    for one in range(4):
        for head in range(2):
            mixed = summed[head] / total[head]
            mixed = mixed.astype(jnp.bfloat16).astype(jnp.float32)
            piece = jnp.where(route_0 == float(one), gate_0 * mixed[0:128, :], 0.0)
            piece = piece + jnp.where(route_1 == float(one), gate_1 * mixed[128:256, :], 0.0)
            pieces.append(piece.astype(jnp.bfloat16))
    for copy in token_copies:
        copy.wait_send()
    for number, piece in enumerate(pieces):
        spread_at = pl.ds(number * 128, 128)
        normed[:, spread_at] = piece
    loads[3].wait()

    def out_tile(tile, carried):
        at = pl.ds(pl.multiple_of(tile * 256, 256), 256)
        partial[:, at] = jnp.dot(
            normed[:, 0:1024], out_weights[:, at], preferred_element_type=jnp.float32
        ).astype(jnp.bfloat16)
        return carried

    lax.fori_loop(0, 8, out_tile, 0)
    part_copies = []
    for step in range(1, 8):
        peer = lax.rem(expert + step, 8)
        copy = send(
            partial.at[pl.ds(pl.multiple_of(peer * 16, 16), 16), :],
            arrived.at[step - 1],
            part_sends,
            part_recvs,
            step - 1,
            (section, seq, peer),
        )
        copy.start()
        part_copies.append(copy)
    result = tokens_ref[section].astype(jnp.float32)
    term = partial[own_rows, :].astype(jnp.float32)
    for step, copy in enumerate(part_copies):
        copy.wait_recv()
        term = term + arrived[step].astype(jnp.float32)
    middle_ref[...] = (result + term).astype(jnp.bfloat16)
    for copy in part_copies:
        copy.wait_send()
    caches.drain()
    freshes.drain()


def attention_stage(
    tokens, lengths, cached, cache, routes, gain, mixing, query_weight, kv_weight, out_weight
):
    depth = tokens.shape[2]
    cache_rows = (
        cache.reshape(2, 256, 2, 2, 128).transpose(0, 1, 3, 2, 4).reshape(2, 1024, 128)
    )
    query_rows = (
        query_weight.reshape(2048, 4, 2, 128).transpose(0, 2, 1, 3).reshape(16384, 128)
    )
    kv_rows = kv_weight.reshape(2048, 2, 2, 128).transpose(0, 2, 1, 3).reshape(8192, 128)
    out_rows = out_weight.reshape(1024, depth)
    vmem = pl.BlockSpec(memory_space=pltpu.VMEM)
    smem = pl.BlockSpec(memory_space=pltpu.SMEM)
    hbm = pl.BlockSpec(memory_space=pl.ANY)
    dma = pltpu.SemaphoreType.DMA
    return pl.pallas_call(
        attention_kernel,
        out_shape=jax.ShapeDtypeStruct((16, depth), jnp.bfloat16),
        in_specs=[smem, smem, vmem, vmem, vmem, vmem, hbm, hbm, hbm, hbm],
        out_specs=vmem,
        scratch_shapes=[
            pltpu.VMEM((1024, 128), jnp.bfloat16),
            pltpu.VMEM((16384, 128), jnp.bfloat16),
            pltpu.VMEM((8192, 128), jnp.bfloat16),
            pltpu.VMEM((2048, 1536), jnp.bfloat16),
            pltpu.VMEM((1024, 2048), jnp.bfloat16),
            pltpu.VMEM((128, 2048), jnp.bfloat16),
            pltpu.VMEM((128, 1536), jnp.float32),
            pltpu.VMEM((8, 4, 256, 128), jnp.bfloat16),
            pltpu.VMEM((8, 4, 128, 128), jnp.bfloat16),
            pltpu.VMEM((2, 256, 128), jnp.bfloat16),
            pltpu.VMEM((2, 256, 128), jnp.float32),
            pltpu.VMEM((2, 256, 128), jnp.float32),
            pltpu.VMEM((2, 256, 128), jnp.float32),
            pltpu.VMEM((128, 2048), jnp.bfloat16),
            pltpu.VMEM((7, 16, 2048), jnp.bfloat16),
            dma((4,)),
            dma((7,)),
            dma((7,)),
            dma((7,)),
            dma((7,)),
            dma((7,)),
            dma((7,)),
            dma((7,)),
            dma((7,)),
        ],
        compiler_params=pltpu.CompilerParams(
            collective_id=0, has_side_effects=True, vmem_limit_bytes=48 << 20
        ),
    )(
        lengths,
        cached,
        tokens,
        routes.transpose(0, 2, 1),
        gain.reshape(1, depth),
        mixing.T,
        cache_rows,
        query_rows,
        kv_rows,
        out_rows,
    )


def expert_hidden(rows, in_weight):
    single = in_weight[0]
    both = jnp.dot(rows, single.reshape(single.shape[0], -1), preferred_element_type=jnp.float32)
    both = both.reshape(rows.shape[0], 2, -1)
    return (jax.nn.silu(both[:, 0]) * both[:, 1]).astype(jnp.bfloat16)


def expert_block(middle, routes, gain, mixing, in_weight, down_weight):
    rows = middle.shape[0]
    features = middle.shape[1]
    normed = rms_scale(middle, gain)
    gates = route_gates(normed, mixing, routes)
    experts = mixing.shape[1]
    capacity = max(2, 4 * rows // experts)
    flat = routes.reshape(-1)
    member = (flat[:, None] == jnp.arange(experts, dtype=jnp.int32)[None, :]).astype(jnp.int32)
    earlier = jnp.cumsum(member, axis=0) - member
    slot = jnp.sum(earlier * member, axis=1)
    target = flat * capacity + slot
    table = (jnp.arange(experts * capacity, dtype=jnp.int32)[:, None] == target[None, :]).astype(
        jnp.bfloat16
    )
    table = jnp.sum(table.reshape(experts * capacity, rows, 2), axis=2)
    buffer = jnp.dot(table, normed, preferred_element_type=jnp.float32).astype(jnp.bfloat16)
    buffer = buffer.reshape(experts, capacity, features)
    seq_count = lax.axis_size("seq")
    copies = jnp.broadcast_to(buffer[None], (seq_count,) + buffer.shape)
    copies = copies.reshape(seq_count * experts, capacity, features)
    arrived = lax.all_to_all(copies, ("seq", "expert"), split_axis=0, concat_axis=0, tiled=True)
    flat_rows = arrived.reshape(-1, features)
    hidden = expert_hidden(flat_rows, in_weight)
    partial_value = jnp.dot(hidden, down_weight[0], preferred_element_type=jnp.float32)
    partial_value = partial_value.astype(jnp.bfloat16).reshape(arrived.shape)
    returned = lax.all_to_all(
        partial_value, ("seq", "expert"), split_axis=0, concat_axis=0, tiled=True
    )
    results = jnp.sum(
        returned.reshape(seq_count, experts, capacity, features).astype(jnp.float32), axis=0
    )
    picked = jnp.take(results.reshape(experts * capacity, features), target, axis=0).reshape(
        rows, 2, features
    )
    mixture = gates[:, 0:1] * picked[:, 0] + gates[:, 1:2] * picked[:, 1]
    return (middle.astype(jnp.float32) + mixture).astype(jnp.bfloat16)


def on_device(
    tokens,
    prompt_lengths,
    cache_lengths,
    kv_cache,
    attn_routes,
    ffn_routes,
    attn_gain,
    ffn_gain,
    attn_mix,
    query_weight,
    kv_weight,
    out_weight,
    ffn_mix,
    in_weight,
    down_weight,
):
    batch = lax.axis_index("section")
    middle = attention_stage(
        tokens,
        prompt_lengths,
        cache_lengths,
        kv_cache,
        attn_routes,
        attn_gain,
        attn_mix,
        query_weight,
        kv_weight,
        out_weight,
    )
    finished = expert_block(
        middle, select_batch(ffn_routes, batch), ffn_gain, ffn_mix, in_weight, down_weight
    )
    return finished[None]


def solution(mesh):
    return jax.shard_map(
        on_device,
        mesh=mesh,
        in_specs=(
            P(None, ("seq", "expert"), None),
            P(),
            P(),
            P(None, "seq", None, "expert"),
            P(None, "seq", None),
            P(None, ("seq", "expert"), None),
            P(),
            P(),
            P(),
            P(None, None, "expert"),
            P(None, None, "expert"),
            P(None, "expert", None),
            P(),
            P("expert", None, None, "seq"),
            P("expert", "seq", None),
        ),
        out_specs=P("section", ("seq", "expert"), None),
        check_vma=False,
    )
```

time: 284 us -> 144 us (0.51)
  waiting for transfers between devices: 123 us -> 27.5 us
  Pallas kernels: 0 us -> 52.1 us
  local copies, waits for them, and re-layouts: 44.3 us -> 11.2 us
  matrix products: 25.3 us -> 6.96 us
  blocking collectives: 53 us -> 36.2 us
  other arithmetic: 18.4 us -> 4.3 us
  between operations: 13.6 us -> 0.16 us
    all_gather x2 -> x0, waiting for transfers between devices: 65.4 us -> none  [the longest x1 60 us: attention_block(): piece = lax.all_gather(cache_rows, 'seq', axis=0, tiled=True)]
    pallas_call x0 -> x1, Pallas kernels: none -> 52.1 us  [attention_stage(): pl.pallas_call(attention_kernel, out_shape=jax.ShapeDtypeStruct((16, dept...]
    reduce_scatter x1 -> x0, waiting for transfers between devices: 30.2 us -> none  [attention_block(): lax.psum_scatter(jnp.dot(spread, out_flat, preferred_element_type=jnp.flo...]
    dot_general x8 -> x0, matrix products: 16 us -> none  [the longest x1 3.73 us: attention_block(): jnp.dot(normed, query_weight.reshape(query_weight.shape[0], -1), preferre...]
    all_gather x1 -> x0, blocking collectives: 15 us -> none  [attention_block(): gathered = lax.all_gather(own_rows, 'expert', axis=0, tiled=True)]
    dot_general x3 -> x0, local copies, waits for them, and re-layouts: 10.9 us -> none  [the longest x2 6.91 us: attention_block(): jnp.dot(normed, query_weight.reshape(query_weight.shape[0], -1), preferre...]
    another operation x6 -> x0, other arithmetic: 4.53 us -> none
    slice x3 -> x0, local copies, waits for them, and re-layouts: 4.5 us -> none  [the longest x1 2.11 us: absorb(): values = piece[:, 1].reshape(-1, local_heads, HEAD_DIM)]
  transfers between devices with their start and end apart: 4 -> 1, of which waited for: 4 -> 1; matrix products, arithmetic and copies ran while one was open for 14% -> 1% of each run, Pallas kernels for 0% -> 0%
where the time goes in v2:
time: 144 us
  Pallas kernels  52.1 us (36%)
  blocking collectives  36.2 us (25%)
  waiting for transfers between devices  27.5 us (19%)
  local copies, waits for them, and re-layouts  11.2 us (8%)
  matrix products  6.96 us (5%)
  starting transfers between devices  5.26 us (4%)
  other arithmetic  4.3 us (3%)
    pallas_call x1, Pallas kernels, attention_stage(): pl.pallas_call(attention_kernel, out_shape=jax.ShapeDtypeStruct((16, dept...  52.1 us
    all_to_all x1, blocking collectives, expert_block(): lax.all_to_all(copies, ('seq', 'expert'), split_axis=0, concat_axis=0, ti...  36.2 us
    all_to_all x1, waiting for transfers between devices, expert_block(): lax.all_to_all(partial_value, ('seq', 'expert'), split_axis=0, concat_axi...  27.5 us
    unnamed x24, local copies, waits for them, and re-layouts  7.01 us
    all_to_all x1, starting transfers between devices, expert_block(): lax.all_to_all(partial_value, ('seq', 'expert'), split_axis=0, concat_axi...  5.26 us
    dot_general x1, matrix products, expert_block(): jnp.dot(hidden, down_weight[0], preferred_element_type=jnp.float32)  3.31 us
    dot_general x1, matrix products, expert_hidden(): jnp.dot(rows, single.reshape(single.shape[0], -1), preferred_element_type...  3.19 us
  transfers between devices with their start and end apart: 1, of which 1 were waited for; matrix products, arithmetic and copies ran while one was open for 1% of the time, Pallas kernels for 0%

profile of v2, /device:TPU:1, one launch (start us, length us, event | category | flops | bytes accessed | tf_op | source)
XLA Modules:
  0.0 143.7 jit_solution(5134931285739729655)
XLA Ops:
  0.0 0.8 fusion.27
  0.9 0.1 reshape.163
  1.1 0.2 select_reduce_fusion
  1.4 0.1 copy.41
  1.6 1.6 %copy-done.1 = bf16[2048,2,256]{2,1,0:T(2,128)(2,1)S(1)} copy-done((bf16[2048,2,256]{2,1,0:T(2,128)(2,1)S(1)}, bf16[2048,2,256]{2,1,0:T(2,128)(2,1)}, u32[]{:S(2)}) %copy-start.1) | copy-done | bytes 2097176
  3.2 1.0 copy-done.2
  4.2 0.9 copy-done.3
  5.1 0.7 copy-done.4
  5.9 0.7 copy-done.5
  6.6 0.7 copy-done.6
  7.2 0.7 copy-done.7
  7.9 0.7 copy-done.8
  8.6 52.1 %shard_map.145 = bf16[16,2048]{1,0:T(8,128)(2,1)S(1)} custom-call(s32[2,3]{1,0:T(2,128)S(1)} %copy-done.7, s32[2,3]{1,0:T(2,128)S(1)} %copy-done.8, bf16[2,16,2048]{2,1,0:T(8,128)(2,1)S(1)} %copy-done.3, s32[2,2,128]{2,1,0:T(2,128)S(1)} %bitcast.92, f32[1,2048]{1,0:T(1,128)S(1)} %bitcast.91, bf16[4,2048]{1,0:T(4,128)(2,1)S(1)} %bitcast.90, ...), custom_call_target="tpu_custom_call" | custom-call | tf_op jit(solution)/shard_map/pallas_call | solution.py:424
  60.7 0.1 fusion.11
  60.9 0.3 fusion.6
  61.2 0.2 broadcast_in_dim.32
  61.4 36.2 %all_to_all.10 = bf16[64,8,2048]{2,1,0:T(8,128)(2,1)S(1)} all-to-all(bf16[64,8,2048]{2,1,0:T(8,128)(2,1)S(1)} %bitcast.94), channel_id=1, replica_groups=mesh['section'=2,'seq'=8,'expert'=8] {'seq','expert'}, dimensions={0} | all-to-all | bytes 4194304 | tf_op jit(solution)/shard_map/all_to_all | solution.py:500
  97.7 3.2 %fusion = f32[512,2,704]{0,2,1:T(8,128)S(1)} fusion(bf16[1,2048,2,704]{1,3,2,0:T(8,128)(2,1)S(1)} %copy-done.10, bf16[64,8,2048]{2,1,0:T(8,128)(2,1)S(1)} %all_to_all.10), kind=kOutput, calls=%fused_computation.2 | convolution fusion | flops 2952790016 | bytes 10747904 | tf_op jit(solution)/shard_map/dot_general | solution.py:474
  100.9 3.3 %fusion.3 = bf16[64,8,2048]{2,1,0:T(8,128)(2,1)} fusion(bf16[1,704,2048]{2,1,0:T(8,128)(2,1)S(1)} %copy-done, f32[512,2,704]{0,2,1:T(8,128)S(1)} %fusion), kind=kOutput, calls=%fused_computation.7 | convolution fusion | flops 1479606272 | bytes 7864320 | tf_op jit(solution)/shard_map/dot_general | solution.py:503
  104.2 5.3 %all-to-all-start.1 = ((bf16[64,8,2048]{2,1,0:T(8,128)(2,1)}), bf16[64,8,2048]{2,1,0:T(8,128)(2,1)}, u32[]{:S(2)}, u32[]{:S(2)}) async-start(bf16[64,8,2048]{2,1,0:T(8,128)(2,1)} %fusion.3), calls=%async_computation.1 | async-start | bytes 4194304 | tf_op jit(solution)/shard_map/all_to_all | solution.py:505
  109.5 0.1 mul.89
  109.6 0.1 copy.38
  109.7 0.1 reshape.177
  109.8 0.2 fusion.22
  110.0 0.7 gather_fusion.1
  110.8 0.1 copy.39
  110.9 27.5 %all-to-all-done.1 = bf16[64,8,2048]{2,1,0:T(8,128)(2,1)} async-done(((bf16[64,8,2048]{2,1,0:T(8,128)(2,1)}), bf16[64,8,2048]{2,1,0:T(8,128)(2,1)}, u32[]{:S(2)}, u32[]{:S(2)}) %all-to-all-start.1) | async-done | bytes 2097184 | tf_op jit(solution)/shard_map/all_to_all | solution.py:505
  138.4 2.0 %convert_reduce_fusion = f32[8,8,2048]{2,1,0:T(8,128)S(1)} fusion(bf16[8,8,8,2048]{3,2,1,0:T(8,128)(2,1)} %bitcast.43), kind=kLoop, calls=%fused_computation.4 | loop fusion | flops 1966080 | bytes 2621440 | tf_op jit(solution)/shard_map/reduce_sum | solution.py:508
  140.4 1.3 gather_fusion
  141.7 1.1 gather.12
  142.8 0.2 copy_select_fusion
  143.0 0.7 fusion.18
  (30 shorter events, 0.6 us)
Async XLA Ops:
  0.0 100.8 %copy-start = (bf16[1,704,2048]{2,1,0:T(8,128)(2,1)S(1)}, bf16[1,704,2048]{2,1,0:T(8,128)(2,1)}, u32[]{:S(2)}) copy-start(bf16[1,704,2048]{2,1,0:T(8,128)(2,1)} %param.29) | copy-start | bytes 8650756
  1.6 1.6 %copy-start.1 = (bf16[2048,2,256]{2,1,0:T(2,128)(2,1)S(1)}, bf16[2048,2,256]{2,1,0:T(2,128)(2,1)}, u32[]{:S(2)}) copy-start(bf16[2048,2,256]{2,1,0:T(2,128)(2,1)} %param.25) | copy-start | bytes 6291460
  3.2 1.0 copy-start.2
  4.2 0.9 copy-start.3
  5.1 0.7 copy-start.4
  5.9 0.7 copy-start.5
  6.6 0.7 copy-start.6
  7.2 0.7 copy-start.7
  7.9 0.7 copy-start.8
  8.6 52.3 %copy-start.9 = (f32[2048]{0:T(1024)S(1)}, f32[2048]{0:T(1024)}, u32[]{:S(2)}) copy-start(f32[2048]{0:T(1024)} %param.22) | copy-start | bytes 24580
  61.2 36.5 %copy-start.10 = (bf16[1,2048,2,704]{1,3,2,0:T(8,128)(2,1)S(1)}, bf16[1,2048,2,704]{1,3,2,0:T(8,128)(2,1)}, u32[]{:S(2)}) copy-start(bf16[1,2048,2,704]{1,3,2,0:T(8,128)(2,1)} %param.28) | copy-start | bytes 17301508
  104.2 5.6 %copy-start.11 = (bf16[2048,8]{0,1:T(8,128)(2,1)S(1)}, bf16[2048,8]{0,1:T(8,128)(2,1)}, u32[]{:S(2)}) copy-start(bf16[2048,8]{0,1:T(8,128)(2,1)} %param.27) | copy-start | bytes 98308
  104.2 34.2 %all-to-all-start.1 = ((bf16[64,8,2048]{2,1,0:T(8,128)(2,1)}), bf16[64,8,2048]{2,1,0:T(8,128)(2,1)}, u32[]{:S(2)}, u32[]{:S(2)}) async-start(bf16[64,8,2048]{2,1,0:T(8,128)(2,1)} %fusion.3), calls=%async_computation.1 | async-start | bytes 4194304 | tf_op jit(solution)/shard_map/all_to_all | solution.py:505
